TPU v7x, 128 devices: a whole 4x4x4 slice. The times are simulated.
128 devices in a mesh: seq: 32 (over z, x, core), head: 4 (over y).
Axes of the slice: x: 4, y: 4, z: 4, core: 2. Of those that a mesh axis runs over, the one named last changes fastest.
Arguments:
- inputs: bfloat16 [32768, 2048], P('seq', 'head'), may hold values from -6 to 6
- w_qkv: bfloat16 [3, 2048, 2048], P(None, None, 'head'), may hold values from -0.125 to 0.125
- level_weight: float32 [16, 6], P('head'), may hold values from 0.5 to 2
- grad_out: bfloat16 [32768, 2048], P('seq', 'head'), may hold values from -6 to 6
Outputs:
- attn_out: bfloat16 [32768, 2048], P('seq', 'head')
- grad_query: bfloat16 [32768, 2048], P('seq', 'head')
- grad_key: bfloat16 [32768, 2048], P('seq', 'head')
- grad_value: bfloat16 [32768, 2048], P('seq', 'head')
All inputs are finite; a program needn't handle non-finite values.
Results may differ from a plain program's by a relative error of at most 0.012.
Values may be sent and summed in bfloat16 or wider, within the bound.
A program may use at most 128 MiB of HBM per device.

v0:
```python
import math

import jax
import jax.numpy as jnp
from jax import lax
from jax.sharding import PartitionSpec as P


def partner(value, axis, stride):
    mask = 2**stride
    pairs = [(source, source ^ mask) for source in range(lax.axis_size(axis))]
    return lax.ppermute(value, axis, pairs)


def per_device(inputs, w_qkv, level_weight, grad_out):
    rows = inputs.shape[0]
    head_count = level_weight.shape[0]
    width = w_qkv.shape[2]
    head_size = width // head_count
    projected = jnp.einsum(
        "tn,jnf->jtf",
        lax.all_gather(inputs, "head", axis=1, tiled=True),
        w_qkv,
        preferred_element_type=jnp.float32,
    ).astype(jnp.bfloat16)
    queries = projected[0].reshape(rows, head_count, head_size)
    keys = projected[1].reshape(rows, head_count, head_size)
    values = projected[2].reshape(rows, head_count, head_size)
    grad_rows = grad_out.reshape(rows, head_count, head_size)
    key_state = jnp.einsum("thd,the->hde", keys, values, preferred_element_type=jnp.float32)
    query_state = jnp.einsum("thd,the->hde", queries, grad_rows, preferred_element_type=jnp.float32)
    position = lax.axis_index("seq")
    depth = lax.axis_size("seq").bit_length() - 1

    def level_coef(bit_level):
        return level_weight[:, bit_level + 1] / math.sqrt(head_size * rows * 2**bit_level)

    forward_mix = jnp.zeros((head_count, head_size, head_size), jnp.float32)
    backward_mix = jnp.zeros((head_count, head_size, head_size), jnp.float32)
    running = key_state
    for bit_level in range(depth):
        partner_sum = partner(running.astype(jnp.bfloat16), "seq", bit_level).astype(running.dtype)
        bit_on = position >> bit_level & 1 == 1
        forward_mix = forward_mix + jnp.where(
            bit_on, level_coef(bit_level)[:, None, None] * partner_sum, 0.0
        )
        running = running + partner_sum
    running = query_state
    for bit_level in range(depth):
        partner_sum = partner(running.astype(jnp.bfloat16), "seq", bit_level).astype(running.dtype)
        bit_on = position >> bit_level & 1 == 1
        backward_mix = backward_mix + jnp.where(
            bit_on, 0.0, level_coef(bit_level)[:, None, None] * partner_sum
        )
        running = running + partner_sum
    forward_low = forward_mix.astype(jnp.bfloat16)
    backward_low = backward_mix.astype(jnp.bfloat16)
    local_scale = (level_weight[:, 0] / math.sqrt(head_size * rows))[:, None, None]
    causal = (jnp.arange(rows)[:, None] >= jnp.arange(rows)[None, :])[None]
    scores = jnp.einsum("thd,shd->hts", queries, keys, preferred_element_type=jnp.float32)
    attend = jnp.where(causal, scores * local_scale, 0.0).astype(jnp.bfloat16)
    grad_scores = jnp.einsum("the,she->hts", grad_rows, values, preferred_element_type=jnp.float32)
    grad_attend = jnp.where(causal, grad_scores * local_scale, 0.0).astype(jnp.bfloat16)
    output = jnp.einsum("hts,she->the", attend, values, preferred_element_type=jnp.float32)
    output = output + jnp.einsum(
        "thd,hde->the", queries, forward_low, preferred_element_type=jnp.float32
    )
    grad_q = jnp.einsum("hts,shd->thd", grad_attend, keys, preferred_element_type=jnp.float32)
    grad_q = grad_q + jnp.einsum(
        "the,hde->thd", grad_rows, forward_low, preferred_element_type=jnp.float32
    )
    grad_k = jnp.einsum("hts,thd->shd", grad_attend, queries, preferred_element_type=jnp.float32)
    grad_k = grad_k + jnp.einsum(
        "the,hde->thd", values, backward_low, preferred_element_type=jnp.float32
    )
    grad_v = jnp.einsum("hts,the->she", attend, grad_rows, preferred_element_type=jnp.float32)
    grad_v = grad_v + jnp.einsum(
        "thd,hde->the", keys, backward_low, preferred_element_type=jnp.float32
    )
    return (
        output.reshape(rows, width).astype(jnp.bfloat16),
        grad_q.reshape(rows, width).astype(jnp.bfloat16),
        grad_k.reshape(rows, width).astype(jnp.bfloat16),
        grad_v.reshape(rows, width).astype(jnp.bfloat16),
    )


def solution(mesh):
    in_specs = (P("seq", "head"), P(None, None, "head"), P("head", None), P("seq", "head"))
    out_specs = (P("seq", "head"), P("seq", "head"), P("seq", "head"), P("seq", "head"))
    return jax.shard_map(
        per_device, mesh=mesh, in_specs=in_specs, out_specs=out_specs, check_vma=False
    )
```

profile of v0, /device:TPU:1, one launch (start us, length us, event | category | flops | bytes accessed | tf_op | source)
XLA Modules:
  0.0 141.7 jit_solution(12768049927329601054)
XLA Ops:
  7.9 1.5 %copy.39 = bf16[1024,512]{0,1:T(8,128)(2,1)S(1)} copy(bf16[1024,512]{1,0:T(8,128)(2,1)} %param.7) | data formatting | bytes 2097152 | tf_op jit(solution)/shard_map/reshape | solution.py:29
  9.4 1.6 %multiply_reduce_fusion.4 = (f32[4]{0:T(128)S(1)}, f32[4]{0:T(128)S(1)}, f32[4]{0:T(128)S(1)}, f32[4]{0:T(128)S(1)}, f32[4]{0:T(128)S(1)}, /*index=5*/f32[4]{0:T(128)}) fusion(f32[4,6]{1,0:T(4,128)} %param.6), kind=kLoop, calls=%fused_computation.56 | loop fusion | flops 24 | bytes 192 | tf_op jit(solution)/shard_map/div | solution.py:36
  12.3 48.6 %all-gather.2.cloned.1.call-done = bf16[1024,2048]{1,0:T(8,128)(2,1)} async-done(((bf16[1024,512]{1,0:T(8,128)(2,1)}), bf16[1024,2048]{1,0:T(8,128)(2,1)}) %all-gather.2.cloned.1.call-update) | async-done | bytes 4194320 | tf_op jit(solution)/shard_map/all_gather | solution.py:22
  60.9 10.3 %convert_bitcast_fusion = bf16[3,1024,512]{1,2,0:T(8,128)(2,1)S(1)} fusion(bf16[3,2048,512]{2,1,0:T(8,128)(2,1)} %param.5, bf16[1024,2048]{1,0:T(8,128)(2,1)} %all-gather.2.cloned.1.call-done), kind=kOutput, calls=%fused_computation.6 | convolution fusion | flops 6444023808 | bytes 13631488 | tf_op jit(solution)/shard_map/tn,jnf->jtf/dot_general | solution.py:20
  72.5 3.1 %fusion = bf16[4,1024,1024]{2,1,0:T(8,128)(2,1)S(1)} fusion(bf16[1024,4,128]{0,2,1:T(8,128)(2,1)S(1)} %bitcast.53, bf16[1024,4,128]{0,2,1:T(8,128)(2,1)S(1)} %bitcast.65, f32[4]{0:T(128)S(1)} %get-tuple-element.11, pred[1024,1024]{1,0:T(8,128)(4,1)S(1)} %copy-done.10), kind=kOutput, calls=%fused_computation.1 | convolution fusion | flops 1086324736 | bytes 11534352 | tf_op jit(solution)/shard_map/the,she->hts/dot_general | solution.py:62
  75.6 2.6 %fusion.42 = f32[4,128,1024]{2,1,0:T(8,128)} fusion(bf16[1024,4,128]{0,2,1:T(8,128)(2,1)S(1)} %bitcast.61, bf16[4,1024,1024]{2,1,0:T(8,128)(2,1)S(1)} %fusion), kind=kOutput, calls=%fused_computation.66 | convolution fusion | flops 1073741824 | bytes 11534336 | tf_op jit(solution)/shard_map/hts,thd->shd/dot_general | solution.py:72
  78.2 2.9 %fusion.41 = f32[4,128,1024]{2,1,0:T(8,128)S(1)} fusion(bf16[1024,4,128]{0,2,1:T(8,128)(2,1)S(1)} %bitcast.57, bf16[4,1024,1024]{2,1,0:T(8,128)(2,1)S(1)} %fusion), kind=kOutput, calls=%fused_computation.65 | convolution fusion | flops 1073741824 | bytes 11534336 | tf_op jit(solution)/shard_map/hts,shd->thd/dot_general | solution.py:68
  81.1 3.1 %select_convert_fusion = bf16[4,1024,1024]{2,1,0:T(8,128)(2,1)S(1)} fusion(bf16[1024,4,128]{0,2,1:T(8,128)(2,1)S(1)} %bitcast.62, bf16[1024,4,128]{0,2,1:T(8,128)(2,1)S(1)} %bitcast.58, f32[4]{0:T(128)S(1)} %get-tuple-element.11, pred[1024,1024]{1,0:T(8,128)(4,1)S(1)} %copy-done.10), kind=kOutput, calls=%fused_computation.2 | convolution fusion | flops 1086324736 | bytes 11534352 | tf_op jit(solution)/shard_map/thd,shd->hts/dot_general | solution.py:60
  85.5 4.3 %fusion.40 = f32[4,128,1024]{2,1,0:T(8,128)} fusion(bf16[1024,4,128]{0,2,1:T(8,128)(2,1)S(1)} %bitcast.66, bf16[4,1024,1024]{2,1,0:T(8,128)(2,1)S(1)} %select_convert_fusion), kind=kOutput, calls=%fused_computation.64 | convolution fusion | flops 1073741824 | bytes 11534336 | tf_op jit(solution)/shard_map/hts,she->the/dot_general | solution.py:64
  91.5 3.3 %collective-permute-done.1 = bf16[4,128,128]{2,1,0:T(8,128)(2,1)S(1)} collective-permute-done((bf16[4,128,128]{2,1,0:T(8,128)(2,1)S(1)}, bf16[4,128,128]{2,1,0:T(8,128)(2,1)S(1)}, u32[]{:S(2)}, u32[]{:S(2)}) %collective-permute-start.1) | collective-permute-done | bytes 131104 | tf_op jit(solution)/shard_map/ppermute | solution.py:12
  94.8 2.8 %collective-permute-start.2 = (bf16[4,128,128]{2,1,0:T(8,128)(2,1)S(1)}, bf16[4,128,128]{2,1,0:T(8,128)(2,1)S(1)}, u32[]{:S(2)}, u32[]{:S(2)}) collective-permute-start(bf16[4,128,128]{2,1,0:T(8,128)(2,1)S(1)} %fusion.30), channel_id=1, source_target_pairs={{0,16},{4,20},{8,24},{12,28},{16,0},{20,4},{24,8},{28,12},{32,48},... | collective-permute-start | bytes 393224 | tf_op jit(solution)/shard_map/ppermute | solution.py:12
  97.6 2.7 %collective-permute-start.7 = (bf16[4,128,128]{2,1,0:T(8,128)(2,1)S(1)}, bf16[4,128,128]{2,1,0:T(8,128)(2,1)S(1)}, u32[]{:S(2)}, u32[]{:S(2)}) collective-permute-start(bf16[4,128,128]{2,1,0:T(8,128)(2,1)S(1)} %fusion.31), channel_id=1, source_target_pairs={{0,16},{4,20},{8,24},{12,28},{16,0},{20,4},{24,8},{28,12},{32,48},... | collective-permute-start | bytes 393224 | tf_op jit(solution)/shard_map/ppermute | solution.py:12
  100.4 1.8 %collective-permute-done.2 = bf16[4,128,128]{2,1,0:T(8,128)(2,1)S(1)} collective-permute-done((bf16[4,128,128]{2,1,0:T(8,128)(2,1)S(1)}, bf16[4,128,128]{2,1,0:T(8,128)(2,1)S(1)}, u32[]{:S(2)}, u32[]{:S(2)}) %collective-permute-start.2) | collective-permute-done | bytes 131104 | tf_op jit(solution)/shard_map/ppermute | solution.py:12
  102.3 1.4 collective-permute-start.3
  104.8 1.4 collective-permute-start.8
  106.3 2.9 %collective-permute-start.4 = (bf16[4,128,128]{2,1,0:T(8,128)(2,1)S(1)}, bf16[4,128,128]{2,1,0:T(8,128)(2,1)S(1)}, u32[]{:S(2)}, u32[]{:S(2)}) collective-permute-start(bf16[4,128,128]{2,1,0:T(8,128)(2,1)S(1)} %fusion.15), channel_id=1, source_target_pairs={{0,64},{4,68},{8,72},{12,76},{16,80},{20,84},{24,88},{28,92},{32,9... | collective-permute-start | bytes 393224 | tf_op jit(solution)/shard_map/ppermute | solution.py:12
  110.9 2.9 %collective-permute-start.9 = (bf16[4,128,128]{2,1,0:T(8,128)(2,1)}, bf16[4,128,128]{2,1,0:T(8,128)(2,1)}, u32[]{:S(2)}, u32[]{:S(2)}) collective-permute-start(bf16[4,128,128]{2,1,0:T(8,128)(2,1)} %fusion.25), channel_id=1, source_target_pairs={{0,64},{4,68},{8,72},{12,76},{16,80},{20,84},{24,88},{28,92},{32,9... | collective-permute-start | bytes 393224 | tf_op jit(solution)/shard_map/ppermute | solution.py:12
  115.1 1.6 %add_convert_fusion.1 = bf16[4,128,1024]{2,1,0:T(8,128)(2,1)} fusion(f32[4,128,1024]{2,1,0:T(8,128)S(1)} %fusion.41, bf16[1024,4,128]{0,2,1:T(8,128)(2,1)S(1)} %bitcast.54, bf16[4,128,128]{2,1,0:T(8,128)(2,1)S(1)} %collective-permute-done, bf16[4,128,128]{2,1,0:T(8,128)(2,1)S(1)} %collective-permute-done.1, ...), kind=kOutput, calls=%fused_computation.10 | convolution fusion | flops 136577024 | bytes 4849749 | tf_op jit(solution)/shard_map/the,hde->thd/dot_general | solution.py:69
  116.7 2.3 %copy.25 = bf16[1024,512]{1,0:T(8,128)(2,1)} copy(bf16[1024,512]{0,1:T(8,128)(2,1)} %bitcast.71) | data formatting | bytes 2097152
  119.0 3.7 %add_convert_fusion = bf16[4,128,1024]{2,1,0:T(8,128)(2,1)} fusion(f32[4,128,1024]{2,1,0:T(8,128)} %fusion.42, bf16[1024,4,128]{0,2,1:T(8,128)(2,1)} %bitcast.67, bf16[4,128,128]{2,1,0:T(8,128)(2,1)S(1)} %collective-permute-done.5, bf16[4,128,128]{2,1,0:T(8,128)(2,1)} %copy-done.3, bf16[4,128,128]{2,1,0:T(8,128)(2,1)} %copy-done.6, ...), kind=kOutput, calls=%fused_computation.9 | convolution fusion | flops 136577024 | bytes 4849749 | tf_op jit(solution)/shard_map/the,hde->thd/dot_general | solution.py:73
  122.7 2.3 %copy.26 = bf16[1024,512]{1,0:T(8,128)(2,1)} copy(bf16[1024,512]{0,1:T(8,128)(2,1)} %bitcast.70) | data formatting | bytes 2097152
  125.0 1.7 %fusion.35 = f32[4,128,1024]{2,1,0:T(8,128)S(1)} fusion(bf16[1024,4,128]{0,2,1:T(8,128)(2,1)S(1)} %bitcast.59, bf16[4,128,128]{2,1,0:T(8,128)(2,1)S(1)} %collective-permute-done.5, bf16[4,128,128]{2,1,0:T(8,128)(2,1)} %copy-done.3, bf16[4,128,128]{2,1,0:T(8,128)(2,1)} %copy-done.6, bf16[4,128,128]{2,1,0:T(8,128)(2,1)} %copy-done.9, ...), kind=kOutput, calls=%fused_computation.63 | convolution fusion | flops 135528448 | bytes 3801173 | tf_op jit(solution)/shard_map/thd,hde->the/dot_general | solution.py:77
  126.7 4.8 %fusion.5 = bf16[1024,4,128]{0,2,1:T(8,128)(2,1)S(1)} fusion(f32[4,128,1024]{2,1,0:T(8,128)S(1)} %fusion.35, bf16[1024,4,128]{0,2,1:T(8,128)(2,1)S(1)} %bitcast.55, bf16[4,1024,1024]{2,1,0:T(8,128)(2,1)} %copy-done), kind=kOutput, calls=%fused_computation.8 | convolution fusion | flops 1074790400 | bytes 12582912 | tf_op jit(solution)/shard_map/hts,the->she/dot_general | solution.py:76
  132.2 1.3 copy.24
  (58 shorter events, 12.6 us)
Async XLA Ops:
  7.2 53.8 %all-gather.2.cloned.1.call-start = ((), (), s32[]{:S(2)}) async-start(), calls=%async_computation | async-start | bytes 5242880 | tf_op jit(solution)/shard_map/all_gather | solution.py:22
  71.6 13.9 %copy-start.1 = (bf16[1,1024,512]{1,2,0:T(8,128)(2,1)}, bf16[1,1024,512]{1,2,0:T(8,128)(2,1)S(1)}, u32[]{:S(2)}) copy-start(bf16[1,1024,512]{1,2,0:T(8,128)(2,1)S(1)} %get-tuple-element.16) | copy-start | bytes 3145732
  84.2 6.9 %copy-start = (bf16[4,1024,1024]{2,1,0:T(8,128)(2,1)}, bf16[4,1024,1024]{2,1,0:T(8,128)(2,1)S(1)}, u32[]{:S(2)}) copy-start(bf16[4,1024,1024]{2,1,0:T(8,128)(2,1)S(1)} %select_convert_fusion) | copy-start | bytes 25165828
  84.2 5.5 %collective-permute-start = (bf16[4,128,128]{2,1,0:T(8,128)(2,1)S(1)}, bf16[4,128,128]{2,1,0:T(8,128)(2,1)S(1)}, u32[]{:S(2)}, u32[]{:S(2)}) collective-permute-start(bf16[4,128,128]{2,1,0:T(8,128)(2,1)S(1)} %get-tuple-element.17), channel_id=1, source_target_pairs={{0,4},{4,0},{8,12},{12,8},{16,20},{20,16},{24,28},{28,24},{32,36},... | collective-permute-start | bytes 393224 | tf_op jit(solution)/shard_map/ppermute | solution.py:12
  85.1 29.9 %copy-start.13 = (f32[4]{0:T(128)S(1)}, f32[4]{0:T(128)}, u32[]{:S(2)}) copy-start(f32[4]{0:T(128)} %get-tuple-element.13) | copy-start | bytes 52
  85.1 5.9 %collective-permute-start.5 = (bf16[4,128,128]{2,1,0:T(8,128)(2,1)S(1)}, bf16[4,128,128]{2,1,0:T(8,128)(2,1)S(1)}, u32[]{:S(2)}, u32[]{:S(2)}) collective-permute-start(bf16[4,128,128]{2,1,0:T(8,128)(2,1)S(1)} %get-tuple-element.19), channel_id=1, source_target_pairs={{0,4},{4,0},{8,12},{12,8},{16,20},{20,16},{24,28},{28,24},{32,36},... | collective-permute-start | bytes 393224 | tf_op jit(solution)/shard_map/ppermute | solution.py:12
  89.8 4.9 %collective-permute-start.1 = (bf16[4,128,128]{2,1,0:T(8,128)(2,1)S(1)}, bf16[4,128,128]{2,1,0:T(8,128)(2,1)S(1)}, u32[]{:S(2)}, u32[]{:S(2)}) collective-permute-start(bf16[4,128,128]{2,1,0:T(8,128)(2,1)S(1)} %fusion.26), channel_id=1, source_target_pairs={{0,8},{4,12},{8,0},{12,4},{16,24},{20,28},{24,16},{28,20},{32,40},... | collective-permute-start | bytes 393224 | tf_op jit(solution)/shard_map/ppermute | solution.py:12
  91.1 6.4 %collective-permute-start.6 = (bf16[4,128,128]{2,1,0:T(8,128)(2,1)S(1)}, bf16[4,128,128]{2,1,0:T(8,128)(2,1)S(1)}, u32[]{:S(2)}, u32[]{:S(2)}) collective-permute-start(bf16[4,128,128]{2,1,0:T(8,128)(2,1)S(1)} %fusion.28), channel_id=1, source_target_pairs={{0,8},{4,12},{8,0},{12,4},{16,24},{20,28},{24,16},{28,20},{32,40},... | collective-permute-start | bytes 393224 | tf_op jit(solution)/shard_map/ppermute | solution.py:12
  94.8 7.4 %collective-permute-start.2 = (bf16[4,128,128]{2,1,0:T(8,128)(2,1)S(1)}, bf16[4,128,128]{2,1,0:T(8,128)(2,1)S(1)}, u32[]{:S(2)}, u32[]{:S(2)}) collective-permute-start(bf16[4,128,128]{2,1,0:T(8,128)(2,1)S(1)} %fusion.30), channel_id=1, source_target_pairs={{0,16},{4,20},{8,24},{12,28},{16,0},{20,4},{24,8},{28,12},{32,48},... | collective-permute-start | bytes 393224 | tf_op jit(solution)/shard_map/ppermute | solution.py:12
  97.6 19.1 %copy-start.3 = (bf16[4,128,128]{2,1,0:T(8,128)(2,1)}, bf16[4,128,128]{2,1,0:T(8,128)(2,1)S(1)}, u32[]{:S(2)}) copy-start(bf16[4,128,128]{2,1,0:T(8,128)(2,1)S(1)} %collective-permute-done.6) | copy-start | bytes 393220
  97.6 7.1 %collective-permute-start.7 = (bf16[4,128,128]{2,1,0:T(8,128)(2,1)S(1)}, bf16[4,128,128]{2,1,0:T(8,128)(2,1)S(1)}, u32[]{:S(2)}, u32[]{:S(2)}) collective-permute-start(bf16[4,128,128]{2,1,0:T(8,128)(2,1)S(1)} %fusion.31), channel_id=1, source_target_pairs={{0,16},{4,20},{8,24},{12,28},{16,0},{20,4},{24,8},{28,12},{32,48},... | collective-permute-start | bytes 393224 | tf_op jit(solution)/shard_map/ppermute | solution.py:12
  102.2 14.4 %copy-start.4 = (bf16[4,128,128]{2,1,0:T(8,128)(2,1)}, bf16[4,128,128]{2,1,0:T(8,128)(2,1)S(1)}, u32[]{:S(2)}) copy-start(bf16[4,128,128]{2,1,0:T(8,128)(2,1)S(1)} %collective-permute-done.2) | copy-start | bytes 393220
  102.3 3.9 %collective-permute-start.3 = (bf16[4,128,128]{2,1,0:T(8,128)(2,1)S(1)}, bf16[4,128,128]{2,1,0:T(8,128)(2,1)S(1)}, u32[]{:S(2)}, u32[]{:S(2)}) collective-permute-start(bf16[4,128,128]{2,1,0:T(8,128)(2,1)S(1)} %fusion.27), channel_id=1, source_target_pairs={{0,32},{4,36},{8,40},{12,44},{16,48},{20,52},{24,56},{28,60},{32,0... | collective-permute-start | bytes 393224 | tf_op jit(solution)/shard_map/ppermute | solution.py:12
  104.7 11.9 %copy-start.6 = (bf16[4,128,128]{2,1,0:T(8,128)(2,1)}, bf16[4,128,128]{2,1,0:T(8,128)(2,1)S(1)}, u32[]{:S(2)}) copy-start(bf16[4,128,128]{2,1,0:T(8,128)(2,1)S(1)} %collective-permute-done.7) | copy-start | bytes 393220
  104.8 5.4 %collective-permute-start.8 = (bf16[4,128,128]{2,1,0:T(8,128)(2,1)S(1)}, bf16[4,128,128]{2,1,0:T(8,128)(2,1)S(1)}, u32[]{:S(2)}, u32[]{:S(2)}) collective-permute-start(bf16[4,128,128]{2,1,0:T(8,128)(2,1)S(1)} %fusion.29), channel_id=1, source_target_pairs={{0,32},{4,36},{8,40},{12,44},{16,48},{20,52},{24,56},{28,60},{32,0... | collective-permute-start | bytes 393224 | tf_op jit(solution)/shard_map/ppermute | solution.py:12
  106.2 10.5 %copy-start.7 = (bf16[4,128,128]{2,1,0:T(8,128)(2,1)}, bf16[4,128,128]{2,1,0:T(8,128)(2,1)S(1)}, u32[]{:S(2)}) copy-start(bf16[4,128,128]{2,1,0:T(8,128)(2,1)S(1)} %collective-permute-done.3) | copy-start | bytes 393220
  106.3 8.8 %collective-permute-start.4 = (bf16[4,128,128]{2,1,0:T(8,128)(2,1)S(1)}, bf16[4,128,128]{2,1,0:T(8,128)(2,1)S(1)}, u32[]{:S(2)}, u32[]{:S(2)}) collective-permute-start(bf16[4,128,128]{2,1,0:T(8,128)(2,1)S(1)} %fusion.15), channel_id=1, source_target_pairs={{0,64},{4,68},{8,72},{12,76},{16,80},{20,84},{24,88},{28,92},{32,9... | collective-permute-start | bytes 393224 | tf_op jit(solution)/shard_map/ppermute | solution.py:12
  110.2 6.5 %copy-start.9 = (bf16[4,128,128]{2,1,0:T(8,128)(2,1)}, bf16[4,128,128]{2,1,0:T(8,128)(2,1)S(1)}, u32[]{:S(2)}) copy-start(bf16[4,128,128]{2,1,0:T(8,128)(2,1)S(1)} %collective-permute-done.8) | copy-start | bytes 393220
  110.9 8.0 %collective-permute-start.9 = (bf16[4,128,128]{2,1,0:T(8,128)(2,1)}, bf16[4,128,128]{2,1,0:T(8,128)(2,1)}, u32[]{:S(2)}, u32[]{:S(2)}) collective-permute-start(bf16[4,128,128]{2,1,0:T(8,128)(2,1)} %fusion.25), channel_id=1, source_target_pairs={{0,64},{4,68},{8,72},{12,76},{16,80},{20,84},{24,88},{28,92},{32,9... | collective-permute-start | bytes 393224 | tf_op jit(solution)/shard_map/ppermute | solution.py:12
  126.7 4.9 %copy-start.2 = (f32[4,128,1024]{2,1,0:T(8,128)S(1)}, f32[4,128,1024]{2,1,0:T(8,128)}, u32[]{:S(2)}) copy-start(f32[4,128,1024]{2,1,0:T(8,128)} %fusion.40) | copy-start | bytes 6291460
  126.7 4.9 %copy-start.5 = (bf16[4,128,128]{2,1,0:T(8,128)(2,1)S(1)}, bf16[4,128,128]{2,1,0:T(8,128)(2,1)}, u32[]{:S(2)}) copy-start(bf16[4,128,128]{2,1,0:T(8,128)(2,1)} %copy-done.4) | copy-start | bytes 393220
  126.7 4.9 %copy-start.8 = (bf16[4,128,128]{2,1,0:T(8,128)(2,1)S(1)}, bf16[4,128,128]{2,1,0:T(8,128)(2,1)}, u32[]{:S(2)}) copy-start(bf16[4,128,128]{2,1,0:T(8,128)(2,1)} %copy-done.7) | copy-start | bytes 393220
  126.7 4.9 %copy-start.12 = (bf16[4,128,128]{2,1,0:T(8,128)(2,1)S(1)}, bf16[4,128,128]{2,1,0:T(8,128)(2,1)}, u32[]{:S(2)}) copy-start(bf16[4,128,128]{2,1,0:T(8,128)(2,1)} %copy-done.11) | copy-start | bytes 393220
  126.7 4.9 %copy-start.14 = (f32[4]{0:T(128)S(1)}, f32[4]{0:T(128)}, u32[]{:S(2)}) copy-start(f32[4]{0:T(128)} %get-tuple-element.13) | copy-start | bytes 52
  (2 other events, 2.8 us)
Sparse Core Ops, SparseCore 0:
  9.6 51.2 all-gather.1
where the time goes:
time: 144 us; the launch traced here: 142 us
  waiting for transfers between devices  57.8 us (40%)
  matrix products  39.6 us (28%)
  starting transfers between devices  16.9 us (12%)
  between operations  14.3 us (10%)
  local copies, waits for them, and re-layouts  9.05 us (6%)
  other arithmetic  4.03 us (3%)
    all_gather x1, waiting for transfers between devices, per_device(): lax.all_gather(inputs, 'head', axis=1, tiled=True)  48.6 us
    ppermute x10, starting transfers between devices, partner(): return lax.ppermute(value, axis, pairs)  16.9 us
    dot_general x1, matrix products, per_device(): jnp.einsum('tn,jnf->jtf', lax.all_gather(inputs, 'head', axis=1, tiled=Tr...  10.3 us
    ppermute x10, waiting for transfers between devices, partner(): return lax.ppermute(value, axis, pairs)  8.48 us
    unnamed x34, local copies, waits for them, and re-layouts  7.26 us
    dot_general x1, matrix products, per_device(): jnp.einsum('hts,the->she', attend, grad_rows, preferred_element_type=jnp....  4.81 us
    dot_general x1, matrix products, per_device(): jnp.einsum('hts,she->the', attend, values, preferred_element_type=jnp.flo...  4.29 us
    dot_general x1, matrix products, per_device(): jnp.einsum('the,hde->thd', values, backward_low, preferred_element_type=j...  3.72 us
  transfers between devices with their start and end apart: 11, of which 6 were waited for; matrix products, arithmetic and copies ran while one was open for 10% of the time, Pallas kernels for 0%

commit v1 on v0

v1 whole, which is shorter than its diff:
```python
import functools
import math

import jax
import jax.numpy as jnp
from jax import lax
from jax.experimental import pallas as pl
from jax.experimental.pallas import tpu as pltpu
from jax.sharding import PartitionSpec as P

MESH = pl.DeviceIdType.MESH
NS = 32
NH = 4
ROWS = 1024
FEAT = 512
HEADS = 4
E = 128
STEPS = 8
ST = ROWS // STEPS
HALF = ST // 2
CHUNKS = 4
T = ROWS // CHUNKS
AHEAD = 4
FAR = 3 * FEAT
F32 = jnp.float32
BF16 = jnp.bfloat16


def dot(a, b):
    return jnp.dot(a, b, preferred_element_type=F32)


def dot_nt(a, b):
    return lax.dot_general(a, b, (((1,), (1,)), ((), ())), preferred_element_type=F32)


def dot_tn(a, b):
    return lax.dot_general(a, b, (((0,), (0,)), ((), ())), preferred_element_type=F32)


def main_kernel(
    x_ref, w_ref, lw_ref, g_ref,
    qkvg, acc, diag,
    xg, wv, pacc, kst, qst, sbuf, rbuf, mix, fbuf,
    own_s, own_r, rel_s, rel_r, loc_sem, w_sem, g_sem, s1, r1, s2, r2,
):
    me = lax.axis_index("seq")
    y = lax.axis_index("head")
    right = lax.rem(y + 1, NH)
    left = lax.rem(y + 3, NH)
    far = lax.rem(y + 2, NH)

    sources = (y, left, right, far)
    w_copies = [
        pltpu.make_async_copy(
            w_ref.at[:, pl.ds(pl.multiple_of(src * FEAT, FEAT), FEAT), :],
            wv.at[:, slot * FEAT : (slot + 1) * FEAT, :],
            w_sem.at[slot],
        )
        for slot, src in enumerate(sources)
    ]
    x_copy = pltpu.make_async_copy(x_ref, xg.at[:, 0:FEAT], loc_sem)
    g_copy = pltpu.make_async_copy(g_ref, qkvg.at[3], g_sem)

    barrier = pltpu.get_barrier_semaphore()
    for other in (left, right):
        pl.semaphore_signal(barrier, inc=1, device_id={"head": other}, device_id_type=MESH)

    def greet(d, c):
        pl.semaphore_signal(
            barrier, inc=1, device_id={"seq": lax.rem(me + d, NS)}, device_id_type=MESH
        )
        return c

    lax.fori_loop(1, NS, greet, 0)
    x_copy.start()
    for copy in w_copies:
        copy.start()
    g_copy.start()
    pl.semaphore_wait(barrier, NS + 1)

    def own(j, way, half):
        rows = pl.ds(pl.multiple_of(j * ST + half * HALF, HALF), HALF)
        return pltpu.make_async_remote_copy(
            src_ref=x_ref.at[rows, :],
            dst_ref=xg.at[rows, (way + 1) * FEAT : (way + 2) * FEAT],
            send_sem=own_s.at[j, way, half],
            recv_sem=own_r.at[j, way, half],
            device_id={"head": right if way == 0 else left},
            device_id_type=MESH,
        )

    def relay(j, way):
        rows = pl.ds(pl.multiple_of(j * ST + way * HALF, HALF), HALF)
        return pltpu.make_async_remote_copy(
            src_ref=xg.at[rows, (way + 1) * FEAT : (way + 2) * FEAT],
            dst_ref=xg.at[rows, FAR : FAR + FEAT],
            send_sem=rel_s.at[j, way],
            recv_sem=rel_r.at[j, way],
            device_id={"head": right if way == 0 else left},
            device_id_type=MESH,
        )

    def start_own(j):
        for half in range(2):
            own(j, 0, half).start()
            own(j, 1, 1 - half).start()

    for j in range(AHEAD):
        start_own(j)
    diag[...] = jnp.zeros_like(diag)
    kst[0] = jnp.zeros((FEAT, E), F32)
    qst[0] = jnp.zeros((FEAT, E), F32)
    x_copy.wait()
    for copy in w_copies:
        copy.wait()
    g_copy.wait()

    def poll(j):
        for way in range(2):
            own(j, way, way).wait_recv()
            relay(j, way).start()

        @pl.when(j + AHEAD < STEPS)
        def _():
            start_own(j + AHEAD)

        for way in range(2):
            own(j, way, 1 - way).wait_recv()

    def chunk_rows(i):
        return pl.ds(pl.multiple_of(i * T, T), T)

    def project_near(i):
        rows = chunk_rows(i)
        for p in range(3):
            pacc[p, rows, :] = dot(xg[rows, 0:FAR], wv[p, 0:FAR, :])

    def project_far(i):
        rows = chunk_rows(i)
        for step in range(2):
            for way in range(2):
                relay(2 * i + step, way).wait_recv()
        for p in range(3):
            full = pacc[p, rows, :] + dot(xg[rows, FAR : FAR + FEAT], wv[p, FAR : FAR + FEAT, :])
            qkvg[p, rows, :] = full.astype(BF16)
        for h in range(HEADS):
            cols = slice(h * E, (h + 1) * E)
            kst[i + 1, cols, :] = kst[i, cols, :] + dot_tn(qkvg[1, rows, cols], qkvg[2, rows, cols])
            qst[i + 1, cols, :] = qst[i, cols, :] + dot_tn(qkvg[0, rows, cols], qkvg[3, rows, cols])

    def local_scale(h):
        return lw_ref[h, 0] * (1.0 / math.sqrt(E * ROWS))

    def attend(i):
        rows = chunk_rows(i)
        at = lax.broadcasted_iota(jnp.int32, (T, T), 0)
        to = lax.broadcasted_iota(jnp.int32, (T, T), 1)
        for h in range(HEADS):
            cols = slice(h * E, (h + 1) * E)
            scale = local_scale(h)
            q, k, v, g = (qkvg[n, rows, cols] for n in range(4))
            before = (kst[i, cols, :] * scale).astype(BF16)
            low = at >= to
            up = at <= to
            a = jnp.where(low, dot_nt(q, k) * scale, 0.0).astype(BF16)
            acc[0, rows, cols] = dot(a, v) + dot(q, before)
            b = jnp.where(low, dot_nt(g, v) * scale, 0.0).astype(BF16)
            acc[1, rows, cols] = dot(b, k) + dot_nt(g, before)
            bt = jnp.where(up, dot_nt(v, g) * scale, 0.0).astype(BF16)
            acc[2, rows, cols] = dot(bt, q)
            a_t = jnp.where(up, dot_nt(k, q) * scale, 0.0).astype(BF16)
            acc[3, rows, cols] = dot(a_t, g)

    def chunk(i, c):
        poll(2 * i)
        poll(2 * i + 1)
        project_near(i)

        @pl.when(i >= 1)
        def _():
            project_far(i - 1)
            attend(i - 1)

        return c

    lax.fori_loop(0, CHUNKS, chunk, 0)
    project_far(CHUNKS - 1)

    sbuf[:, 0:16, :] = kst[CHUNKS].reshape(NS, 16, E).astype(BF16)
    sbuf[:, 16:32, :] = qst[CHUNKS].reshape(NS, 16, E).astype(BF16)

    def give(p):
        return pltpu.make_async_remote_copy(
            src_ref=sbuf.at[p], dst_ref=rbuf.at[me], send_sem=s1.at[p], recv_sem=r1.at[me],
            device_id={"seq": p}, device_id_type=MESH,
        )

    def take(p):
        return pltpu.make_async_remote_copy(
            src_ref=sbuf.at[p], dst_ref=rbuf.at[p], send_sem=s1.at[p], recv_sem=r1.at[p],
            device_id={"seq": p}, device_id_type=MESH,
        )

    def give_mix(p):
        return pltpu.make_async_remote_copy(
            src_ref=mix.at[p], dst_ref=fbuf.at[me], send_sem=s2.at[p], recv_sem=r2.at[me],
            device_id={"seq": p}, device_id_type=MESH,
        )

    def take_mix(p):
        return pltpu.make_async_remote_copy(
            src_ref=mix.at[p], dst_ref=fbuf.at[p], send_sem=s2.at[p], recv_sem=r2.at[p],
            device_id={"seq": p}, device_id_type=MESH,
        )

    def others(fn):
        def body(d, c):
            fn(lax.rem(me + d, NS))
            return c

        lax.fori_loop(1, NS, body, 0)

    others(lambda p: give(p).start())
    rbuf[me] = sbuf[me]

    attend(CHUNKS - 1)

    def later(i, c):
        rows = chunk_rows(i)
        for h in range(HEADS):
            cols = slice(h * E, (h + 1) * E)
            after = ((qst[CHUNKS, cols, :] - qst[i + 1, cols, :]) * local_scale(h)).astype(BF16)
            acc[2, rows, cols] += dot_nt(qkvg[2, rows, cols], after)
            acc[3, rows, cols] += dot(qkvg[1, rows, cols], after)
        return c

    lax.fori_loop(0, CHUNKS - 1, later, 0)

    others(lambda p: take(p).wait_recv())
    head = me // (NS // HEADS)
    coef = [lw_ref[head, b + 1] * (1.0 / math.sqrt(E * ROWS * 2**b)) for b in range(5)]
    for part in range(2):
        part_rows = slice(part * 16, part * 16 + 16)
        sums = [rbuf[c, part_rows, :].astype(F32) for c in range(NS)]
        total = [None] * NS
        for b in range(5):
            for c in range(NS):
                bit = c >> b & 1
                if bit == 1 - part:
                    term = coef[b] * sums[(c >> b) ^ 1]
                    total[c] = term if total[c] is None else total[c] + term
            sums = [sums[2 * n] + sums[2 * n + 1] for n in range(len(sums) // 2)]
        for c in range(NS):
            value = jnp.zeros((16, E), F32) if total[c] is None else total[c]
            mix[c, part_rows, :] = value.astype(BF16)
    others(lambda p: give_mix(p).start())
    fbuf[me] = mix[me]
    for j in range(STEPS):
        for way in range(2):
            relay(j, way).wait_send()
            for half in range(2):
                own(j, way, half).wait_send()
    others(lambda p: give(p).wait_send())
    others(lambda p: take_mix(p).wait_recv())
    for h in range(HEADS):
        pair, side = h // 2, h % 2
        span = slice(side * E, (side + 1) * E)
        for part in range(2):
            block = fbuf[8 * h : 8 * h + 8, part * 16 : part * 16 + 16, :].reshape(E, E)
            diag[part, pair, span, span] = block
    others(lambda p: give_mix(p).wait_send())


def finish_kernel(qkvg, acc, diag, o_ref, gq_ref, gk_ref, gv_ref, buf, sem):
    outs = (o_ref, gq_ref, gk_ref, gv_ref)
    plan = ((0, 0, dot), (3, 0, dot_nt), (2, 1, dot_nt), (1, 1, dot))
    copies = []
    for i in range(CHUNKS):
        rows = slice(i * T, (i + 1) * T)
        for n, (lhs, part, fn) in enumerate(plan):
            for pair in range(2):
                cols = slice(pair * 2 * E, (pair + 1) * 2 * E)
                value = acc[n, rows, cols] + fn(qkvg[lhs, rows, cols], diag[part, pair])
                buf[n, rows, cols] = value.astype(BF16)
            copy = pltpu.make_async_copy(buf.at[n, rows, :], outs[n].at[rows, :], sem.at[n, i])
            copy.start()
            copies.append(copy)
    for copy in copies:
        copy.wait()


def per_device(inputs, w_qkv, level_weight, grad_out):
    any_spec = pl.BlockSpec(memory_space=pl.ANY)
    vmem = pl.BlockSpec(memory_space=pltpu.VMEM)
    dma = pltpu.SemaphoreType.DMA
    qkvg, acc, diag = pl.pallas_call(
        main_kernel,
        out_shape=(
            pltpu.VMEM((4, ROWS, FEAT), BF16),
            pltpu.VMEM((4, ROWS, FEAT), F32),
            pltpu.VMEM((2, 2, 2 * E, 2 * E), BF16),
        ),
        in_specs=[any_spec, any_spec, pl.BlockSpec(memory_space=pltpu.SMEM), any_spec],
        out_specs=(vmem, vmem, vmem),
        scratch_shapes=[
            pltpu.VMEM((ROWS, 4 * FEAT), BF16),
            pltpu.VMEM((3, 4 * FEAT, FEAT), BF16),
            pltpu.VMEM((3, ROWS, FEAT), F32),
            pltpu.VMEM((CHUNKS + 1, FEAT, E), F32),
            pltpu.VMEM((CHUNKS + 1, FEAT, E), F32),
            pltpu.VMEM((NS, 32, E), BF16),
            pltpu.VMEM((NS, 32, E), BF16),
            pltpu.VMEM((NS, 32, E), BF16),
            pltpu.VMEM((NS, 32, E), BF16),
            dma((STEPS, 2, 2)),
            dma((STEPS, 2, 2)),
            dma((STEPS, 2)),
            dma((STEPS, 2)),
            dma(()),
            dma((4,)),
            dma(()),
            dma((NS,)),
            dma((NS,)),
            dma((NS,)),
            dma((NS,)),
        ],
        compiler_params=pltpu.CompilerParams(
            collective_id=0, has_side_effects=True, vmem_limit_bytes=36 * 2**20
        ),
        name="gather_and_mix",
    )(inputs, w_qkv, level_weight, grad_out)
    out = jax.ShapeDtypeStruct((ROWS, FEAT), BF16)
    return pl.pallas_call(
        finish_kernel,
        out_shape=(out, out, out, out),
        in_specs=[vmem, vmem, vmem],
        out_specs=(any_spec,) * 4,
        scratch_shapes=[pltpu.VMEM((4, ROWS, FEAT), BF16), dma((4, CHUNKS))],
        name="finish",
    )(qkvg, acc, diag)


def solution(mesh):
    in_specs = (P("seq", "head"), P(None, None, "head"), P("head", None), P("seq", "head"))
    out_specs = (P("seq", "head"), P("seq", "head"), P("seq", "head"), P("seq", "head"))
    return jax.shard_map(
        per_device, mesh=mesh, in_specs=in_specs, out_specs=out_specs, check_vma=False
    )
```

time: 144 us -> 78.1 us (0.54); the launches traced: 142 us -> 77.9 us
  Pallas kernels: 0 us -> 68.1 us
  waiting for transfers between devices: 57.8 us -> 0 us
  matrix products: 39.6 us -> 0 us
  starting transfers between devices: 16.9 us -> 0 us
  between operations: 14.3 us -> 0.66 us
  other arithmetic: 4.03 us -> 0 us
    pallas_call x0 -> x2, Pallas kernels: none -> 68.1 us  [the longest x1 61.1 us: per_device(): pl.pallas_call(main_kernel, out_shape=(pltpu.VMEM((4, ROWS, FEAT), BF16),...]
    all_gather x1 -> x0, waiting for transfers between devices: 48.6 us -> none  [per_device(): lax.all_gather(inputs, 'head', axis=1, tiled=True)]
    dot_general x13 -> x0, matrix products: 39.6 us -> none  [the longest x1 10.3 us: per_device(): jnp.einsum('tn,jnf->jtf', lax.all_gather(inputs, 'head', axis=1, tiled=Tr...]
    ppermute x10 -> x0, starting transfers between devices: 16.9 us -> none  [partner(): return lax.ppermute(value, axis, pairs)]
    ppermute x10 -> x0, waiting for transfers between devices: 8.48 us -> none  [partner(): return lax.ppermute(value, axis, pairs)]
    unnamed x34 -> x12, local copies, waits for them, and re-layouts: 7.26 us -> 9.12 us
    div x1 -> x0, other arithmetic: 1.61 us -> none  [level_coef(): level_weight[:, bit_level + 1]]
    reshape x1 -> x0, local copies, waits for them, and re-layouts: 1.49 us -> none  [per_device(): grad_rows = grad_out.reshape(rows, head_count, head_size)]
  transfers between devices with their start and end apart: 11 -> 0, of which waited for: 6 -> 0; matrix products, arithmetic and copies ran while one was open for 10% -> 0% of each run, Pallas kernels for 0% -> 0%
where the time goes in v1:
time: 78.1 us; the launch traced here: 77.9 us
  Pallas kernels  68.1 us (87%)
  local copies, waits for them, and re-layouts  9.12 us (12%)
    pallas_call x1, Pallas kernels, per_device(): pl.pallas_call(main_kernel, out_shape=(pltpu.VMEM((4, ROWS, FEAT), BF16),...  61.1 us
    unnamed x12, local copies, waits for them, and re-layouts  9.12 us
    pallas_call x1, Pallas kernels, per_device(): pl.pallas_call(finish_kernel, out_shape=(out, out, out, out), in_specs=[v...  6.99 us

profile of v1, /device:TPU:1, one launch (start us, length us, event | category | flops | bytes accessed | tf_op | source)
XLA Modules:
  0.0 77.9 jit_solution(10291945650851739213)
XLA Ops:
  0.6 0.0 copy-start.2
  0.6 1.2 %copy-done.2 = bf16[1024,512]{1,0:T(8,128)(2,1)S(1)} copy-done((bf16[1024,512]{1,0:T(8,128)(2,1)S(1)}, bf16[1024,512]{1,0:T(8,128)(2,1)}, u32[]{:S(2)}) %copy-start.2) | copy-done | bytes 1048600
  1.9 0.0 copy-start.3
  1.9 1.2 %copy-done.3 = bf16[1024,512]{1,0:T(8,128)(2,1)S(1)} copy-done((bf16[1024,512]{1,0:T(8,128)(2,1)S(1)}, bf16[1024,512]{1,0:T(8,128)(2,1)}, u32[]{:S(2)}) %copy-start.3) | copy-done | bytes 1048600
  3.1 0.0 copy-start.5
  3.1 0.7 copy-done.5
  3.8 61.1 %gather_and_mix.1 = (bf16[4,1024,512]{2,1,0:T(8,128)(2,1)S(1)}, f32[4,1024,512]{2,1,0:T(8,128)S(1)}, bf16[2,2,256,256]{3,2,1,0:T(8,128)(2,1)S(1)}) custom-call(bf16[1024,512]{1,0:T(8,128)(2,1)S(1)} %copy-done.2, bf16[3,2048,512]{2,1,0:T(8,128)(2,1)} %w_ref.1, f32[4,6]{1,0:T(4,128)S(1)} %copy-done.5, bf16[1024,512]{1,0:T(8,128)(2,1)S(1)} %copy-done.3), custom_call_target="tpu_custom_call" | custom-call | tf_op jit(solution)/shard_map/gather_and_mix/pallas_call | solution.py:297
  64.9 0.0 copy-start
  64.9 3.2 %copy-done = f32[4,1024,512]{2,1,0:T(8,128)} copy-done((f32[4,1024,512]{2,1,0:T(8,128)}, f32[4,1024,512]{2,1,0:T(8,128)S(1)}, u32[]{:S(2)}) %copy-start) | copy-done | bytes 8388632
  68.1 0.0 copy-start.1
  68.1 2.0 %copy-done.1 = bf16[4,1024,512]{2,1,0:T(8,128)(2,1)} copy-done((bf16[4,1024,512]{2,1,0:T(8,128)(2,1)}, bf16[4,1024,512]{2,1,0:T(8,128)(2,1)S(1)}, u32[]{:S(2)}) %copy-start.1) | copy-done | bytes 4194328
  70.1 0.0 copy-start.4
  70.1 0.8 %copy-done.4 = bf16[2,2,256,256]{3,2,1,0:T(8,128)(2,1)} copy-done((bf16[2,2,256,256]{3,2,1,0:T(8,128)(2,1)}, bf16[2,2,256,256]{3,2,1,0:T(8,128)(2,1)S(1)}, u32[]{:S(2)}) %copy-start.4) | copy-done | bytes 524312
  70.9 7.0 %finish.1 = (bf16[1024,512]{1,0:T(8,128)(2,1)}, bf16[1024,512]{1,0:T(8,128)(2,1)}, bf16[1024,512]{1,0:T(8,128)(2,1)}, bf16[1024,512]{1,0:T(8,128)(2,1)}) custom-call(bf16[4,1024,512]{2,1,0:T(8,128)(2,1)} %copy-done.1, f32[4,1024,512]{2,1,0:T(8,128)} %copy-done, bf16[2,2,256,256]{3,2,1,0:T(8,128)(2,1)} %copy-done.4), custom_call_target="tpu_custom_call" | custom-call | tf_op jit(solution)/shard_map/finish/pallas_call | solution.py:334
Async XLA Ops:
  0.6 1.2 %copy-start.2 = (bf16[1024,512]{1,0:T(8,128)(2,1)S(1)}, bf16[1024,512]{1,0:T(8,128)(2,1)}, u32[]{:S(2)}) copy-start(bf16[1024,512]{1,0:T(8,128)(2,1)} %x_ref.1) | copy-start | bytes 3145732
  1.9 1.2 %copy-start.3 = (bf16[1024,512]{1,0:T(8,128)(2,1)S(1)}, bf16[1024,512]{1,0:T(8,128)(2,1)}, u32[]{:S(2)}) copy-start(bf16[1024,512]{1,0:T(8,128)(2,1)} %g_ref.1) | copy-start | bytes 3145732
  3.1 0.7 copy-start.5
  64.9 3.2 %copy-start = (f32[4,1024,512]{2,1,0:T(8,128)}, f32[4,1024,512]{2,1,0:T(8,128)S(1)}, u32[]{:S(2)}) copy-start(f32[4,1024,512]{2,1,0:T(8,128)S(1)} %get-tuple-element.8.acc) | copy-start | bytes 25165828
  68.1 2.0 %copy-start.1 = (bf16[4,1024,512]{2,1,0:T(8,128)(2,1)}, bf16[4,1024,512]{2,1,0:T(8,128)(2,1)S(1)}, u32[]{:S(2)}) copy-start(bf16[4,1024,512]{2,1,0:T(8,128)(2,1)S(1)} %get-tuple-element.7.qkvg) | copy-start | bytes 12582916
  70.1 0.8 %copy-start.4 = (bf16[2,2,256,256]{3,2,1,0:T(8,128)(2,1)}, bf16[2,2,256,256]{3,2,1,0:T(8,128)(2,1)S(1)}, u32[]{:S(2)}) copy-start(bf16[2,2,256,256]{3,2,1,0:T(8,128)(2,1)S(1)} %get-tuple-element.9.diag) | copy-start | bytes 1572868

commit v2 on v1

--- a/solution.py
+++ b/solution.py
@@ -39,10 +39,10 @@
 
 
 def main_kernel(
-    x_ref, w_ref, lw_ref, g_ref,
+    x_ref, w_ref, lw_hbm, g_ref,
     qkvg, acc, diag,
     xg, wv, pacc, kst, qst, sbuf, rbuf, mix, fbuf,
-    own_s, own_r, rel_s, rel_r, loc_sem, w_sem, g_sem, s1, r1, s2, r2,
+    own_s, own_r, rel_s, rel_r, loc_sem, w_sem, g_sem, s1, r1, s2, r2, lw_ref, lw_sem,
 ):
     me = lax.axis_index("seq")
     y = lax.axis_index("head")
@@ -61,6 +61,7 @@
     ]
     x_copy = pltpu.make_async_copy(x_ref, xg.at[:, 0:FEAT], loc_sem)
     g_copy = pltpu.make_async_copy(g_ref, qkvg.at[3], g_sem)
+    lw_copy = pltpu.make_async_copy(lw_hbm, lw_ref, lw_sem)
 
     barrier = pltpu.get_barrier_semaphore()
     for other in (left, right):
@@ -77,6 +78,7 @@
     for copy in w_copies:
         copy.start()
     g_copy.start()
+    lw_copy.start()
     pl.semaphore_wait(barrier, NS + 1)
 
     def own(j, way, half):
@@ -115,6 +117,7 @@
     for copy in w_copies:
         copy.wait()
     g_copy.wait()
+    lw_copy.wait()
 
     def poll(j):
         for way in range(2):
@@ -291,6 +294,7 @@
 
 
 def per_device(inputs, w_qkv, level_weight, grad_out):
+    place = pltpu.with_memory_space_constraint
     any_spec = pl.BlockSpec(memory_space=pl.ANY)
     vmem = pl.BlockSpec(memory_space=pltpu.VMEM)
     dma = pltpu.SemaphoreType.DMA
@@ -301,7 +305,7 @@
             pltpu.VMEM((4, ROWS, FEAT), F32),
             pltpu.VMEM((2, 2, 2 * E, 2 * E), BF16),
         ),
-        in_specs=[any_spec, any_spec, pl.BlockSpec(memory_space=pltpu.SMEM), any_spec],
+        in_specs=[any_spec] * 4,
         out_specs=(vmem, vmem, vmem),
         scratch_shapes=[
             pltpu.VMEM((ROWS, 4 * FEAT), BF16),
@@ -324,12 +328,14 @@
             dma((NS,)),
             dma((NS,)),
             dma((NS,)),
+            pltpu.SMEM((HEADS, 6), F32),
+            dma(()),
         ],
         compiler_params=pltpu.CompilerParams(
             collective_id=0, has_side_effects=True, vmem_limit_bytes=36 * 2**20
         ),
         name="gather_and_mix",
-    )(inputs, w_qkv, level_weight, grad_out)
+    )(*(place(a, pltpu.MemorySpace.HBM) for a in (inputs, w_qkv, level_weight, grad_out)))
     out = jax.ShapeDtypeStruct((ROWS, FEAT), BF16)
     return pl.pallas_call(
         finish_kernel,
@@ -337,8 +343,9 @@
         in_specs=[vmem, vmem, vmem],
         out_specs=(any_spec,) * 4,
         scratch_shapes=[pltpu.VMEM((4, ROWS, FEAT), BF16), dma((4, CHUNKS))],
+        compiler_params=pltpu.CompilerParams(vmem_limit_bytes=8 * 2**20),
         name="finish",
-    )(qkvg, acc, diag)
+    )(*(place(a, pltpu.MemorySpace.VMEM) for a in (qkvg, acc, diag)))
 
 
 def solution(mesh):

time: 78.1 us -> 64 us (0.82)
  local copies, waits for them, and re-layouts: 9.12 us -> 0 us
  Pallas kernels: 68.1 us -> 63.2 us
    unnamed x12 -> x0, local copies, waits for them, and re-layouts: 9.12 us -> none
    pallas_call x1, Pallas kernels: 6.99 us -> 2.37 us  [per_device(): pl.pallas_call(finish_kernel, out_shape=(out, out, out, out), in_specs=[v...]
where the time goes in v2:
time: 64 us; the launch traced here: 63.8 us
  Pallas kernels  63.2 us (99%)
  between operations  0.64 us (1%)
    pallas_call x1, Pallas kernels, per_device(): pl.pallas_call(main_kernel, out_shape=(pltpu.VMEM((4, ROWS, FEAT), BF16),...  60.8 us
    pallas_call x1, Pallas kernels, per_device(): pl.pallas_call(finish_kernel, out_shape=(out, out, out, out), in_specs=[v...  2.37 us

profile of v2, /device:TPU:1, one launch (start us, length us, event | category | flops | bytes accessed | tf_op | source)
XLA Modules:
  0.0 63.8 jit_solution(683321160851544644)
XLA Ops:
  0.6 60.8 %gather_and_mix.1 = (bf16[4,1024,512]{2,1,0:T(8,128)(2,1)S(1)}, f32[4,1024,512]{2,1,0:T(8,128)S(1)}, bf16[2,2,256,256]{3,2,1,0:T(8,128)(2,1)S(1)}) custom-call(bf16[1024,512]{1,0:T(8,128)(2,1)} %x_ref.1, bf16[3,2048,512]{2,1,0:T(8,128)(2,1)} %w_ref.1, f32[4,6]{1,0:T(4,128)} %lw_hbm.1, bf16[1024,512]{1,0:T(8,128)(2,1)} %g_ref.1), custom_call_target="tpu_custom_call" | custom-call | tf_op jit(solution)/shard_map/gather_and_mix/pallas_call | solution.py:301
  61.5 2.4 %finish.1 = (bf16[1024,512]{1,0:T(8,128)(2,1)}, bf16[1024,512]{1,0:T(8,128)(2,1)}, bf16[1024,512]{1,0:T(8,128)(2,1)}, bf16[1024,512]{1,0:T(8,128)(2,1)}) custom-call(bf16[4,1024,512]{2,1,0:T(8,128)(2,1)S(1)} %get-tuple-element.7.qkvg, f32[4,1024,512]{2,1,0:T(8,128)S(1)} %get-tuple-element.8.acc, bf16[2,2,256,256]{3,2,1,0:T(8,128)(2,1)S(1)} %get-tuple-element.9.diag), custom_call_target="tpu_custom_call" | custom-call | tf_op jit(solution)/shard_map/finish/pallas_call | solution.py:340

commit v3 on v2

--- a/solution.py
+++ b/solution.py
@@ -42,7 +42,7 @@
     x_ref, w_ref, lw_hbm, g_ref,
     qkvg, acc, diag,
     xg, wv, pacc, kst, qst, sbuf, rbuf, mix, fbuf,
-    own_s, own_r, rel_s, rel_r, loc_sem, w_sem, g_sem, s1, r1, s2, r2, lw_ref, lw_sem,
+    own_s, own_r, rel_s, rel_r, loc_sem, w_sem, g_sem, s1, r1, s2, r2, lw_ref, lw_sem, word,
 ):
     me = lax.axis_index("seq")
     y = lax.axis_index("head")
@@ -63,23 +63,33 @@
     g_copy = pltpu.make_async_copy(g_ref, qkvg.at[3], g_sem)
     lw_copy = pltpu.make_async_copy(lw_hbm, lw_ref, lw_sem)
 
+    core = lax.rem(me, 2)
+    along_x = lax.rem(me // 2, 4)
+    along_z = me // 8
+
+    def at_offset(dz, dx, dc):
+        z = lax.rem(along_z + dz, 4) * 8
+        x = lax.rem(along_x + dx, 4) * 2
+        return z + x + (core if dc == 0 else 1 - core)
+
+    x_peers = [at_offset(0, d, 0) for d in (1, 3)]
+    z_peers = [at_offset(d, 0, 0) for d in (1, 3)]
+    partner = at_offset(0, 0, 1)
     barrier = pltpu.get_barrier_semaphore()
-    for other in (left, right):
-        pl.semaphore_signal(barrier, inc=1, device_id={"head": other}, device_id_type=MESH)
-
-    def greet(d, c):
-        pl.semaphore_signal(
-            barrier, inc=1, device_id={"seq": lax.rem(me + d, NS)}, device_id_type=MESH
-        )
-        return c
-
-    lax.fori_loop(1, NS, greet, 0)
+
+    def signal(sem, axis, device):
+        pl.semaphore_signal(sem, inc=1, device_id={axis: device}, device_id_type=MESH)
+
+    for device in (left, right):
+        signal(barrier, "head", device)
+    for device in (*x_peers, *z_peers, partner):
+        signal(barrier, "seq", device)
     x_copy.start()
     for copy in w_copies:
         copy.start()
     g_copy.start()
     lw_copy.start()
-    pl.semaphore_wait(barrier, NS + 1)
+    pl.semaphore_wait(barrier, 7)
 
     def own(j, way, half):
         rows = pl.ds(pl.multiple_of(j * ST + half * HALF, HALF), HALF)
@@ -110,6 +120,10 @@
 
     for j in range(AHEAD):
         start_own(j)
+    for n, peers in enumerate((x_peers, z_peers, z_peers, [partner])):
+        for device in peers:
+            signal(word.at[n], "seq", device)
+        pl.semaphore_wait(word.at[n], len(peers))
     diag[...] = jnp.zeros_like(diag)
     kst[0] = jnp.zeros((FEAT, E), F32)
     qst[0] = jnp.zeros((FEAT, E), F32)
@@ -193,38 +207,28 @@
     sbuf[:, 0:16, :] = kst[CHUNKS].reshape(NS, 16, E).astype(BF16)
     sbuf[:, 16:32, :] = qst[CHUNKS].reshape(NS, 16, E).astype(BF16)
 
-    def give(p):
-        return pltpu.make_async_remote_copy(
-            src_ref=sbuf.at[p], dst_ref=rbuf.at[me], send_sem=s1.at[p], recv_sem=r1.at[me],
+    steps = sorted(
+        ((dz, dx, dc) for dz in range(4) for dx in range(4) for dc in range(2)),
+        key=lambda o: -min(o[0], 4 - o[0]) - min(o[1], 4 - o[1]) - o[2] / 2,
+    )[:-1]
+    peers = [at_offset(*step) for step in steps]
+    gives = [
+        pltpu.make_async_remote_copy(
+            src_ref=sbuf.at[p], dst_ref=rbuf.at[me], send_sem=s1.at[n], recv_sem=r1.at[n],
             device_id={"seq": p}, device_id_type=MESH,
         )
-
-    def take(p):
-        return pltpu.make_async_remote_copy(
-            src_ref=sbuf.at[p], dst_ref=rbuf.at[p], send_sem=s1.at[p], recv_sem=r1.at[p],
+        for n, p in enumerate(peers)
+    ]
+    give_mixes = [
+        pltpu.make_async_remote_copy(
+            src_ref=mix.at[p], dst_ref=fbuf.at[me], send_sem=s2.at[n], recv_sem=r2.at[n],
             device_id={"seq": p}, device_id_type=MESH,
         )
-
-    def give_mix(p):
-        return pltpu.make_async_remote_copy(
-            src_ref=mix.at[p], dst_ref=fbuf.at[me], send_sem=s2.at[p], recv_sem=r2.at[me],
-            device_id={"seq": p}, device_id_type=MESH,
-        )
-
-    def take_mix(p):
-        return pltpu.make_async_remote_copy(
-            src_ref=mix.at[p], dst_ref=fbuf.at[p], send_sem=s2.at[p], recv_sem=r2.at[p],
-            device_id={"seq": p}, device_id_type=MESH,
-        )
-
-    def others(fn):
-        def body(d, c):
-            fn(lax.rem(me + d, NS))
-            return c
-
-        lax.fori_loop(1, NS, body, 0)
-
-    others(lambda p: give(p).start())
+        for n, p in enumerate(peers)
+    ]
+
+    for copy in gives:
+        copy.start()
     rbuf[me] = sbuf[me]
 
     attend(CHUNKS - 1)
@@ -240,7 +244,8 @@
 
     lax.fori_loop(0, CHUNKS - 1, later, 0)
 
-    others(lambda p: take(p).wait_recv())
+    for copy in gives:
+        copy.wait_recv()
     head = me // (NS // HEADS)
     coef = [lw_ref[head, b + 1] * (1.0 / math.sqrt(E * ROWS * 2**b)) for b in range(5)]
     for part in range(2):
@@ -257,22 +262,26 @@
         for c in range(NS):
             value = jnp.zeros((16, E), F32) if total[c] is None else total[c]
             mix[c, part_rows, :] = value.astype(BF16)
-    others(lambda p: give_mix(p).start())
+    for copy in give_mixes:
+        copy.start()
     fbuf[me] = mix[me]
     for j in range(STEPS):
         for way in range(2):
             relay(j, way).wait_send()
             for half in range(2):
                 own(j, way, half).wait_send()
-    others(lambda p: give(p).wait_send())
-    others(lambda p: take_mix(p).wait_recv())
+    for copy in gives:
+        copy.wait_send()
+    for copy in give_mixes:
+        copy.wait_recv()
     for h in range(HEADS):
         pair, side = h // 2, h % 2
         span = slice(side * E, (side + 1) * E)
         for part in range(2):
             block = fbuf[8 * h : 8 * h + 8, part * 16 : part * 16 + 16, :].reshape(E, E)
             diag[part, pair, span, span] = block
-    others(lambda p: give_mix(p).wait_send())
+    for copy in give_mixes:
+        copy.wait_send()
 
 
 def finish_kernel(qkvg, acc, diag, o_ref, gq_ref, gk_ref, gv_ref, buf, sem):
@@ -330,6 +339,7 @@
             dma((NS,)),
             pltpu.SMEM((HEADS, 6), F32),
             dma(()),
+            pltpu.SemaphoreType.REGULAR((4,)),
         ],
         compiler_params=pltpu.CompilerParams(
             collective_id=0, has_side_effects=True, vmem_limit_bytes=36 * 2**20

time: 64 us -> 60.9 us (0.952)
  Pallas kernels: 63.2 us -> 60.1 us
    pallas_call x1, Pallas kernels: 60.8 us -> 57.8 us  [per_device(): pl.pallas_call(main_kernel, out_shape=(pltpu.VMEM((4, ROWS, FEAT), BF16),...]
where the time goes in v3:
time: 60.9 us; the launch traced here: 60.8 us
  Pallas kernels  60.1 us (99%)
  between operations  0.64 us (1%)
    pallas_call x1, Pallas kernels, per_device(): pl.pallas_call(main_kernel, out_shape=(pltpu.VMEM((4, ROWS, FEAT), BF16),...  57.8 us
    pallas_call x1, Pallas kernels, per_device(): pl.pallas_call(finish_kernel, out_shape=(out, out, out, out), in_specs=[v...  2.37 us

profile of v3, /device:TPU:1, one launch (start us, length us, event | category | flops | bytes accessed | tf_op | source)
XLA Modules:
  0.0 60.8 jit_solution(15167715436111844672)
XLA Ops:
  0.6 57.8 %gather_and_mix.1 = (bf16[4,1024,512]{2,1,0:T(8,128)(2,1)S(1)}, f32[4,1024,512]{2,1,0:T(8,128)S(1)}, bf16[2,2,256,256]{3,2,1,0:T(8,128)(2,1)S(1)}) custom-call(bf16[1024,512]{1,0:T(8,128)(2,1)} %x_ref.1, bf16[3,2048,512]{2,1,0:T(8,128)(2,1)} %w_ref.1, f32[4,6]{1,0:T(4,128)} %lw_hbm.1, bf16[1024,512]{1,0:T(8,128)(2,1)} %g_ref.1), custom_call_target="tpu_custom_call" | custom-call | tf_op jit(solution)/shard_map/gather_and_mix/pallas_call | solution.py:310
  58.4 2.4 %finish.1 = (bf16[1024,512]{1,0:T(8,128)(2,1)}, bf16[1024,512]{1,0:T(8,128)(2,1)}, bf16[1024,512]{1,0:T(8,128)(2,1)}, bf16[1024,512]{1,0:T(8,128)(2,1)}) custom-call(bf16[4,1024,512]{2,1,0:T(8,128)(2,1)S(1)} %get-tuple-element.7.qkvg, f32[4,1024,512]{2,1,0:T(8,128)S(1)} %get-tuple-element.8.acc, bf16[2,2,256,256]{3,2,1,0:T(8,128)(2,1)S(1)} %get-tuple-element.9.diag), custom_call_target="tpu_custom_call" | custom-call | tf_op jit(solution)/shard_map/finish/pallas_call | solution.py:350

commit v4 on v3

--- a/solution.py
+++ b/solution.py
@@ -22,6 +22,8 @@
 T = ROWS // CHUNKS
 AHEAD = 4
 FAR = 3 * FEAT
+CHIPS = NS // 2
+SLICE = FEAT // CHIPS
 F32 = jnp.float32
 BF16 = jnp.bfloat16
 
@@ -154,17 +156,33 @@
             pacc[p, rows, :] = dot(xg[rows, 0:FAR], wv[p, 0:FAR, :])
 
     def project_far(i):
-        rows = chunk_rows(i)
-        for step in range(2):
-            for way in range(2):
-                relay(2 * i + step, way).wait_recv()
-        for p in range(3):
+        for h in range(HEADS):
+            cols = slice(h * E, (h + 1) * E)
+            kst[i + 1, cols, :] = kst[i, cols, :]
+            qst[i + 1, cols, :] = qst[i, cols, :]
+        far_step(i, 0)
+
+        @pl.when(i < CHUNKS - 1)
+        def _():
+            far_step(i, 1)
+
+    def far_step(i, step):
+        rows = pl.ds(pl.multiple_of(i * T + step * ST, ST), ST)
+        for way in range(2):
+            relay(2 * i + step, way).wait_recv()
+        project(rows, (0, 1, 2))
+        add_states(i, rows, kst, 1, 2)
+        add_states(i, rows, qst, 0, 3)
+
+    def project(rows, parts):
+        for p in parts:
             full = pacc[p, rows, :] + dot(xg[rows, FAR : FAR + FEAT], wv[p, FAR : FAR + FEAT, :])
             qkvg[p, rows, :] = full.astype(BF16)
+
+    def add_states(i, rows, states, a, b):
         for h in range(HEADS):
             cols = slice(h * E, (h + 1) * E)
-            kst[i + 1, cols, :] = kst[i, cols, :] + dot_tn(qkvg[1, rows, cols], qkvg[2, rows, cols])
-            qst[i + 1, cols, :] = qst[i, cols, :] + dot_tn(qkvg[0, rows, cols], qkvg[3, rows, cols])
+            states[i + 1, cols, :] += dot_tn(qkvg[a, rows, cols], qkvg[b, rows, cols])
 
     def local_scale(h):
         return lw_ref[h, 0] * (1.0 / math.sqrt(E * ROWS))
@@ -204,32 +222,55 @@
     lax.fori_loop(0, CHUNKS, chunk, 0)
     project_far(CHUNKS - 1)
 
-    sbuf[:, 0:16, :] = kst[CHUNKS].reshape(NS, 16, E).astype(BF16)
-    sbuf[:, 16:32, :] = qst[CHUNKS].reshape(NS, 16, E).astype(BF16)
-
-    steps = sorted(
+    chip = me // 2
+    offsets = sorted(
         ((dz, dx, dc) for dz in range(4) for dx in range(4) for dc in range(2)),
-        key=lambda o: -min(o[0], 4 - o[0]) - min(o[1], 4 - o[1]) - o[2] / 2,
+        key=lambda o: (-o[2], -min(o[0], 4 - o[0]) - min(o[1], 4 - o[1])),
     )[:-1]
-    peers = [at_offset(*step) for step in steps]
-    gives = [
-        pltpu.make_async_remote_copy(
-            src_ref=sbuf.at[p], dst_ref=rbuf.at[me], send_sem=s1.at[n], recv_sem=r1.at[n],
-            device_id={"seq": p}, device_id_type=MESH,
+    peers = [at_offset(*offset) for offset in offsets]
+    gives = []
+    give_mixes = []
+    for n, (offset, peer) in enumerate(zip(offsets, peers)):
+        owned = core if offset[2] == 0 else 1 - core
+        gives.append(
+            pltpu.make_async_remote_copy(
+                src_ref=sbuf.at[owned, peer // 2], dst_ref=rbuf.at[me],
+                send_sem=s1.at[n], recv_sem=r1.at[n],
+                device_id={"seq": peer}, device_id_type=MESH,
+            )
         )
-        for n, p in enumerate(peers)
-    ]
-    give_mixes = [
-        pltpu.make_async_remote_copy(
-            src_ref=mix.at[p], dst_ref=fbuf.at[me], send_sem=s2.at[n], recv_sem=r2.at[n],
-            device_id={"seq": p}, device_id_type=MESH,
+        give_mixes.append(
+            pltpu.make_async_remote_copy(
+                src_ref=mix.at[peer], dst_ref=fbuf.at[core, chip],
+                send_sem=s2.at[n], recv_sem=r2.at[n],
+                device_id={"seq": peer}, device_id_type=MESH,
+            )
         )
-        for n, p in enumerate(peers)
-    ]
-
-    for copy in gives:
-        copy.start()
-    rbuf[me] = sbuf[me]
+
+    last = slice(ROWS - ST, ROWS)
+    for way in range(2):
+        relay(STEPS - 1, way).wait_recv()
+
+    def last_step(kind, states, a, b, parts):
+        project(last, parts)
+        add_states(CHUNKS - 1, last, states, a, b)
+        sbuf[kind] = states[CHUNKS].reshape(CHIPS, SLICE, E).astype(BF16)
+
+    keys = (0, kst, 1, 2, (1, 2))
+    queries = (1, qst, 0, 3, (0,))
+    for n in range(2):
+
+        @pl.when(core == 1 - n)
+        def _():
+            last_step(*keys)
+
+        @pl.when(core == n)
+        def _():
+            last_step(*queries)
+
+        for copy in gives[n * CHIPS : (n + 1) * CHIPS]:
+            copy.start()
+    rbuf[me] = sbuf[core, chip]
 
     attend(CHUNKS - 1)
 
@@ -246,25 +287,23 @@
 
     for copy in gives:
         copy.wait_recv()
-    head = me // (NS // HEADS)
-    coef = [lw_ref[head, b + 1] * (1.0 / math.sqrt(E * ROWS * 2**b)) for b in range(5)]
-    for part in range(2):
-        part_rows = slice(part * 16, part * 16 + 16)
-        sums = [rbuf[c, part_rows, :].astype(F32) for c in range(NS)]
-        total = [None] * NS
-        for b in range(5):
-            for c in range(NS):
-                bit = c >> b & 1
-                if bit == 1 - part:
-                    term = coef[b] * sums[(c >> b) ^ 1]
-                    total[c] = term if total[c] is None else total[c] + term
-            sums = [sums[2 * n] + sums[2 * n + 1] for n in range(len(sums) // 2)]
+    def place_of(c):
+        return c + core * (NS - 1 - 2 * c)
+
+    head = chip // (CHIPS // HEADS)
+    sums = [rbuf[place_of(c)].astype(F32) for c in range(NS)]
+    total = [jnp.zeros((SLICE, E), F32)] * NS
+    for b in range(5):
+        coef = lw_ref[head, b + 1] * (1.0 / math.sqrt(E * ROWS * 2**b))
         for c in range(NS):
-            value = jnp.zeros((16, E), F32) if total[c] is None else total[c]
-            mix[c, part_rows, :] = value.astype(BF16)
+            if c >> b & 1:
+                total[c] = total[c] + coef * sums[(c >> b) ^ 1]
+        sums = [sums[2 * n] + sums[2 * n + 1] for n in range(len(sums) // 2)]
+    for c in range(NS):
+        mix[place_of(c)] = total[c].astype(BF16)
     for copy in give_mixes:
         copy.start()
-    fbuf[me] = mix[me]
+    fbuf[core, chip] = mix[me]
     for j in range(STEPS):
         for way in range(2):
             relay(j, way).wait_send()
@@ -274,11 +313,13 @@
         copy.wait_send()
     for copy in give_mixes:
         copy.wait_recv()
+
+    per_head = CHIPS // HEADS
     for h in range(HEADS):
         pair, side = h // 2, h % 2
         span = slice(side * E, (side + 1) * E)
         for part in range(2):
-            block = fbuf[8 * h : 8 * h + 8, part * 16 : part * 16 + 16, :].reshape(E, E)
+            block = fbuf[part, h * per_head : (h + 1) * per_head].reshape(E, E)
             diag[part, pair, span, span] = block
     for copy in give_mixes:
         copy.wait_send()
@@ -307,7 +348,7 @@
     any_spec = pl.BlockSpec(memory_space=pl.ANY)
     vmem = pl.BlockSpec(memory_space=pltpu.VMEM)
     dma = pltpu.SemaphoreType.DMA
-    qkvg, acc, diag = pl.pallas_call(
+    state = pl.pallas_call(
         main_kernel,
         out_shape=(
             pltpu.VMEM((4, ROWS, FEAT), BF16),
@@ -315,17 +356,17 @@
             pltpu.VMEM((2, 2, 2 * E, 2 * E), BF16),
         ),
         in_specs=[any_spec] * 4,
-        out_specs=(vmem, vmem, vmem),
+        out_specs=(vmem,) * 3,
         scratch_shapes=[
             pltpu.VMEM((ROWS, 4 * FEAT), BF16),
             pltpu.VMEM((3, 4 * FEAT, FEAT), BF16),
             pltpu.VMEM((3, ROWS, FEAT), F32),
             pltpu.VMEM((CHUNKS + 1, FEAT, E), F32),
             pltpu.VMEM((CHUNKS + 1, FEAT, E), F32),
-            pltpu.VMEM((NS, 32, E), BF16),
-            pltpu.VMEM((NS, 32, E), BF16),
-            pltpu.VMEM((NS, 32, E), BF16),
-            pltpu.VMEM((NS, 32, E), BF16),
+            pltpu.VMEM((2, CHIPS, SLICE, E), BF16),
+            pltpu.VMEM((NS, SLICE, E), BF16),
+            pltpu.VMEM((NS, SLICE, E), BF16),
+            pltpu.VMEM((2, CHIPS, SLICE, E), BF16),
             dma((STEPS, 2, 2)),
             dma((STEPS, 2, 2)),
             dma((STEPS, 2)),
@@ -350,12 +391,12 @@
     return pl.pallas_call(
         finish_kernel,
         out_shape=(out, out, out, out),
-        in_specs=[vmem, vmem, vmem],
+        in_specs=[vmem] * 3,
         out_specs=(any_spec,) * 4,
         scratch_shapes=[pltpu.VMEM((4, ROWS, FEAT), BF16), dma((4, CHUNKS))],
         compiler_params=pltpu.CompilerParams(vmem_limit_bytes=8 * 2**20),
         name="finish",
-    )(*(place(a, pltpu.MemorySpace.VMEM) for a in (qkvg, acc, diag)))
+    )(*(place(a, pltpu.MemorySpace.VMEM) for a in state))
 
 
 def solution(mesh):

time: 60.9 us -> 60.6 us (level)
  no operation moved by 1% of the time
where the time goes in v4:
time: 60.6 us; the launch traced here: 60.5 us
  Pallas kernels  59.8 us (99%)
  between operations  0.64 us (1%)
    pallas_call x1, Pallas kernels, per_device(): pl.pallas_call(main_kernel, out_shape=(pltpu.VMEM((4, ROWS, FEAT), BF16),...  57.5 us
    pallas_call x1, Pallas kernels, per_device(): pl.pallas_call(finish_kernel, out_shape=(out, out, out, out), in_specs=[v...  2.37 us

profile of v4, /device:TPU:1, one launch (start us, length us, event | category | flops | bytes accessed | tf_op | source)
XLA Modules:
  0.0 60.5 jit_solution(4989488896139002408)
XLA Ops:
  0.6 57.5 %gather_and_mix.1 = (bf16[4,1024,512]{2,1,0:T(8,128)(2,1)S(1)}, f32[4,1024,512]{2,1,0:T(8,128)S(1)}, bf16[2,2,256,256]{3,2,1,0:T(8,128)(2,1)S(1)}) custom-call(bf16[1024,512]{1,0:T(8,128)(2,1)} %x_ref.1, bf16[3,2048,512]{2,1,0:T(8,128)(2,1)} %w_ref.1, f32[4,6]{1,0:T(4,128)} %lw_hbm.1, bf16[1024,512]{1,0:T(8,128)(2,1)} %g_ref.1), custom_call_target="tpu_custom_call" | custom-call | tf_op jit(solution)/shard_map/gather_and_mix/pallas_call | solution.py:351
  58.1 2.4 %finish.1 = (bf16[1024,512]{1,0:T(8,128)(2,1)}, bf16[1024,512]{1,0:T(8,128)(2,1)}, bf16[1024,512]{1,0:T(8,128)(2,1)}, bf16[1024,512]{1,0:T(8,128)(2,1)}) custom-call(bf16[4,1024,512]{2,1,0:T(8,128)(2,1)S(1)} %get-tuple-element.7.qkvg, f32[4,1024,512]{2,1,0:T(8,128)S(1)} %get-tuple-element.8.acc, bf16[2,2,256,256]{3,2,1,0:T(8,128)(2,1)S(1)} %get-tuple-element.9.diag), custom_call_target="tpu_custom_call" | custom-call | tf_op jit(solution)/shard_map/finish/pallas_call | solution.py:391

commit v5 on v4

--- a/solution.py
+++ b/solution.py
@@ -20,7 +20,7 @@
 HALF = ST // 2
 CHUNKS = 4
 T = ROWS // CHUNKS
-AHEAD = 4
+AHEAD = 2
 FAR = 3 * FEAT
 CHIPS = NS // 2
 SLICE = FEAT // CHIPS
@@ -93,13 +93,13 @@
     lw_copy.start()
     pl.semaphore_wait(barrier, 7)
 
-    def own(j, way, half):
-        rows = pl.ds(pl.multiple_of(j * ST + half * HALF, HALF), HALF)
+    def own(i, way):
+        rows = pl.ds(pl.multiple_of(i * T, T), T)
         return pltpu.make_async_remote_copy(
             src_ref=x_ref.at[rows, :],
             dst_ref=xg.at[rows, (way + 1) * FEAT : (way + 2) * FEAT],
-            send_sem=own_s.at[j, way, half],
-            recv_sem=own_r.at[j, way, half],
+            send_sem=own_s.at[i, way],
+            recv_sem=own_r.at[i, way],
             device_id={"head": right if way == 0 else left},
             device_id_type=MESH,
         )
@@ -115,13 +115,12 @@
             device_id_type=MESH,
         )
 
-    def start_own(j):
-        for half in range(2):
-            own(j, 0, half).start()
-            own(j, 1, 1 - half).start()
-
-    for j in range(AHEAD):
-        start_own(j)
+    def start_own(i):
+        for way in range(2):
+            own(i, way).start()
+
+    for i in range(AHEAD):
+        start_own(i)
     for n, peers in enumerate((x_peers, z_peers, z_peers, [partner])):
         for device in peers:
             signal(word.at[n], "seq", device)
@@ -135,17 +134,15 @@
     g_copy.wait()
     lw_copy.wait()
 
-    def poll(j):
+    def poll(i):
         for way in range(2):
-            own(j, way, way).wait_recv()
-            relay(j, way).start()
-
-        @pl.when(j + AHEAD < STEPS)
-        def _():
-            start_own(j + AHEAD)
-
-        for way in range(2):
-            own(j, way, 1 - way).wait_recv()
+            own(i, way).wait_recv()
+            for step in range(T // ST):
+                relay(i * (T // ST) + step, way).start()
+
+        @pl.when(i + AHEAD < CHUNKS)
+        def _():
+            start_own(i + AHEAD)
 
     def chunk_rows(i):
         return pl.ds(pl.multiple_of(i * T, T), T)
@@ -208,13 +205,15 @@
             acc[3, rows, cols] = dot(a_t, g)
 
     def chunk(i, c):
-        poll(2 * i)
-        poll(2 * i + 1)
+        poll(i)
         project_near(i)
 
         @pl.when(i >= 1)
         def _():
             project_far(i - 1)
+
+        @pl.when((i >= 1) & (i < CHUNKS - 1))
+        def _():
             attend(i - 1)
 
         return c
@@ -272,18 +271,7 @@
             copy.start()
     rbuf[me] = sbuf[core, chip]
 
-    attend(CHUNKS - 1)
-
-    def later(i, c):
-        rows = chunk_rows(i)
-        for h in range(HEADS):
-            cols = slice(h * E, (h + 1) * E)
-            after = ((qst[CHUNKS, cols, :] - qst[i + 1, cols, :]) * local_scale(h)).astype(BF16)
-            acc[2, rows, cols] += dot_nt(qkvg[2, rows, cols], after)
-            acc[3, rows, cols] += dot(qkvg[1, rows, cols], after)
-        return c
-
-    lax.fori_loop(0, CHUNKS - 1, later, 0)
+    attend(CHUNKS - 2)
 
     for copy in gives:
         copy.wait_recv()
@@ -304,11 +292,25 @@
     for copy in give_mixes:
         copy.start()
     fbuf[core, chip] = mix[me]
+    attend(CHUNKS - 1)
+
+    def later(i, c):
+        rows = chunk_rows(i)
+        for h in range(HEADS):
+            cols = slice(h * E, (h + 1) * E)
+            after = ((qst[CHUNKS, cols, :] - qst[i + 1, cols, :]) * local_scale(h)).astype(BF16)
+            acc[2, rows, cols] += dot_nt(qkvg[2, rows, cols], after)
+            acc[3, rows, cols] += dot(qkvg[1, rows, cols], after)
+        return c
+
+    lax.fori_loop(0, CHUNKS - 1, later, 0)
+
     for j in range(STEPS):
         for way in range(2):
             relay(j, way).wait_send()
-            for half in range(2):
-                own(j, way, half).wait_send()
+    for i in range(CHUNKS):
+        for way in range(2):
+            own(i, way).wait_send()
     for copy in gives:
         copy.wait_send()
     for copy in give_mixes:
@@ -367,8 +369,8 @@
             pltpu.VMEM((NS, SLICE, E), BF16),
             pltpu.VMEM((NS, SLICE, E), BF16),
             pltpu.VMEM((2, CHIPS, SLICE, E), BF16),
-            dma((STEPS, 2, 2)),
-            dma((STEPS, 2, 2)),
+            dma((CHUNKS, 2)),
+            dma((CHUNKS, 2)),
             dma((STEPS, 2)),
             dma((STEPS, 2)),
             dma(()),

time: 60.6 us -> 59 us (0.974)
  Pallas kernels: 59.8 us -> 58.2 us
    pallas_call x1, Pallas kernels: 57.5 us -> 55.8 us  [per_device(): pl.pallas_call(main_kernel, out_shape=(pltpu.VMEM((4, ROWS, FEAT), BF16),...]
where the time goes in v5:
time: 59 us; the launch traced here: 58.8 us
  Pallas kernels  58.2 us (99%)
  between operations  0.64 us (1%)
    pallas_call x1, Pallas kernels, per_device(): pl.pallas_call(main_kernel, out_shape=(pltpu.VMEM((4, ROWS, FEAT), BF16),...  55.8 us
    pallas_call x1, Pallas kernels, per_device(): pl.pallas_call(finish_kernel, out_shape=(out, out, out, out), in_specs=[v...  2.37 us

profile of v5, /device:TPU:1, one launch (start us, length us, event | category | flops | bytes accessed | tf_op | source)
XLA Modules:
  0.0 58.8 jit_solution(9202286549934765224)
XLA Ops:
  0.6 55.8 %gather_and_mix.1 = (bf16[4,1024,512]{2,1,0:T(8,128)(2,1)S(1)}, f32[4,1024,512]{2,1,0:T(8,128)S(1)}, bf16[2,2,256,256]{3,2,1,0:T(8,128)(2,1)S(1)}) custom-call(bf16[1024,512]{1,0:T(8,128)(2,1)} %x_ref.1, bf16[3,2048,512]{2,1,0:T(8,128)(2,1)} %w_ref.1, f32[4,6]{1,0:T(4,128)} %lw_hbm.1, bf16[1024,512]{1,0:T(8,128)(2,1)} %g_ref.1), custom_call_target="tpu_custom_call" | custom-call | tf_op jit(solution)/shard_map/gather_and_mix/pallas_call | solution.py:353
  56.5 2.4 %finish.1 = (bf16[1024,512]{1,0:T(8,128)(2,1)}, bf16[1024,512]{1,0:T(8,128)(2,1)}, bf16[1024,512]{1,0:T(8,128)(2,1)}, bf16[1024,512]{1,0:T(8,128)(2,1)}) custom-call(bf16[4,1024,512]{2,1,0:T(8,128)(2,1)S(1)} %get-tuple-element.7.qkvg, f32[4,1024,512]{2,1,0:T(8,128)S(1)} %get-tuple-element.8.acc, bf16[2,2,256,256]{3,2,1,0:T(8,128)(2,1)S(1)} %get-tuple-element.9.diag), custom_call_target="tpu_custom_call" | custom-call | tf_op jit(solution)/shard_map/finish/pallas_call | solution.py:393

commit v6 on v5

--- a/solution.py
+++ b/solution.py
@@ -115,6 +115,17 @@
             device_id_type=MESH,
         )
 
+    def relay_chunk(i, way):
+        rows = pl.ds(pl.multiple_of(i * T + way * ST, ST), ST)
+        return pltpu.make_async_remote_copy(
+            src_ref=xg.at[rows, (way + 1) * FEAT : (way + 2) * FEAT],
+            dst_ref=xg.at[rows, FAR : FAR + FEAT],
+            send_sem=rel_s.at[2 * i, way],
+            recv_sem=rel_r.at[2 * i, way],
+            device_id={"head": right if way == 0 else left},
+            device_id_type=MESH,
+        )
+
     def start_own(i):
         for way in range(2):
             own(i, way).start()
@@ -137,8 +148,15 @@
     def poll(i):
         for way in range(2):
             own(i, way).wait_recv()
-            for step in range(T // ST):
-                relay(i * (T // ST) + step, way).start()
+
+            @pl.when(i < CHUNKS - 1)
+            def _():
+                relay_chunk(i, way).start()
+
+            @pl.when(i == CHUNKS - 1)
+            def _():
+                for step in range(T // ST):
+                    relay(i * (T // ST) + step, way).start()
 
         @pl.when(i + AHEAD < CHUNKS)
         def _():
@@ -157,6 +175,17 @@
             cols = slice(h * E, (h + 1) * E)
             kst[i + 1, cols, :] = kst[i, cols, :]
             qst[i + 1, cols, :] = qst[i, cols, :]
+
+        @pl.when(i < CHUNKS - 1)
+        def _():
+            for way in range(2):
+                relay_chunk(i, way).wait_recv()
+
+        @pl.when(i == CHUNKS - 1)
+        def _():
+            for way in range(2):
+                relay(2 * i, way).wait_recv()
+
         far_step(i, 0)
 
         @pl.when(i < CHUNKS - 1)
@@ -165,8 +194,6 @@
 
     def far_step(i, step):
         rows = pl.ds(pl.multiple_of(i * T + step * ST, ST), ST)
-        for way in range(2):
-            relay(2 * i + step, way).wait_recv()
         project(rows, (0, 1, 2))
         add_states(i, rows, kst, 1, 2)
         add_states(i, rows, qst, 0, 3)
@@ -212,7 +239,7 @@
         def _():
             project_far(i - 1)
 
-        @pl.when((i >= 1) & (i < CHUNKS - 1))
+        @pl.when(i == 1)
         def _():
             attend(i - 1)
 
@@ -271,7 +298,7 @@
             copy.start()
     rbuf[me] = sbuf[core, chip]
 
-    attend(CHUNKS - 2)
+    lax.fori_loop(1, CHUNKS - 1, lambda i, c: (attend(i), c)[1], 0)
 
     for copy in gives:
         copy.wait_recv()
@@ -305,8 +332,10 @@
 
     lax.fori_loop(0, CHUNKS - 1, later, 0)
 
-    for j in range(STEPS):
-        for way in range(2):
+    for way in range(2):
+        for i in range(CHUNKS - 1):
+            relay_chunk(i, way).wait_send()
+        for j in range(STEPS - 2, STEPS):
             relay(j, way).wait_send()
     for i in range(CHUNKS):
         for way in range(2):

time: 59 us -> 59.1 us (level)
  no operation moved by 1% of the time
where the time goes in v6:
time: 59.1 us; the launch traced here: 59 us
  Pallas kernels  58.4 us (99%)
  between operations  0.64 us (1%)
    pallas_call x1, Pallas kernels, per_device(): pl.pallas_call(main_kernel, out_shape=(pltpu.VMEM((4, ROWS, FEAT), BF16),...  56 us
    pallas_call x1, Pallas kernels, per_device(): pl.pallas_call(finish_kernel, out_shape=(out, out, out, out), in_specs=[v...  2.37 us

profile of v6, /device:TPU:1, one launch (start us, length us, event | category | flops | bytes accessed | tf_op | source)
XLA Modules:
  0.0 59.0 jit_solution(8711806333939582716)
XLA Ops:
  0.6 56.0 %gather_and_mix.1 = (bf16[4,1024,512]{2,1,0:T(8,128)(2,1)S(1)}, f32[4,1024,512]{2,1,0:T(8,128)S(1)}, bf16[2,2,256,256]{3,2,1,0:T(8,128)(2,1)S(1)}) custom-call(bf16[1024,512]{1,0:T(8,128)(2,1)} %x_ref.1, bf16[3,2048,512]{2,1,0:T(8,128)(2,1)} %w_ref.1, f32[4,6]{1,0:T(4,128)} %lw_hbm.1, bf16[1024,512]{1,0:T(8,128)(2,1)} %g_ref.1), custom_call_target="tpu_custom_call" | custom-call | tf_op jit(solution)/shard_map/gather_and_mix/pallas_call | solution.py:382
  56.7 2.4 %finish.1 = (bf16[1024,512]{1,0:T(8,128)(2,1)}, bf16[1024,512]{1,0:T(8,128)(2,1)}, bf16[1024,512]{1,0:T(8,128)(2,1)}, bf16[1024,512]{1,0:T(8,128)(2,1)}) custom-call(bf16[4,1024,512]{2,1,0:T(8,128)(2,1)S(1)} %get-tuple-element.7.qkvg, f32[4,1024,512]{2,1,0:T(8,128)S(1)} %get-tuple-element.8.acc, bf16[2,2,256,256]{3,2,1,0:T(8,128)(2,1)S(1)} %get-tuple-element.9.diag), custom_call_target="tpu_custom_call" | custom-call | tf_op jit(solution)/shard_map/finish/pallas_call | solution.py:422
